TPU v7x, 256 devices: a whole 4x4x8 slice. The times are simulated.
256 devices in a mesh: leaf: 64 (over x, z, core), rhs: 4 (over y).
Axes of the slice: x: 4, y: 4, z: 8, core: 2. Of those that a mesh axis runs over, the one named last changes fastest.
Arguments:
- input_columns: float32 [8, 1024, 256], P('rhs', 'leaf'), may hold values from -6 to 6
- near_blocks: float32 [8192, 256, 256], P(('leaf', 'rhs')), may hold values from -0.25 to 0.25
- near_pairs: int32 [8192, 2], P(('leaf', 'rhs')), may hold values from -1 to 1023, as said below
- leaf_basis: float32 [1024, 64, 256], P(('leaf', 'rhs')), may hold values from -0.375 to 0.375
- local_transfer: float32 [1792, 64, 64], P('leaf'), may hold values from -0.5 to 0.5
- local_coupling: float32 [1792, 4, 64, 64], P('leaf'), may hold values from -0.4375 to 0.4375
- local_lists: int32 [1792, 4], P('leaf'), may hold values from -1 to 1023, as said below
- middle_transfer: float32 [128, 64, 64], P('leaf'), may hold values from -0.5 to 0.5
- middle_coupling: float32 [192, 4, 64, 64], P('leaf'), may hold values from -0.75 to 0.75
- middle_lists: int32 [192, 4], P('leaf'), may hold values from -1 to 127, as said below
- upper_transfer: float32 [126, 64, 64], replicated, may hold values from -0.5 to 0.5
- upper_coupling: float32 [64, 4, 64, 64], P('leaf'), may hold values from -1 to 1
- upper_lists: int32 [64, 4], P('leaf'), may hold values from -1 to 31, as said below
Outputs:
- first_product: float32 [8, 1024, 256], P(None, ('leaf', 'rhs'))
- second_product: float32 [8, 1024, 256], P(None, ('leaf', 'rhs'))
Inputs may be any that keep to these rules, and one draw needn't show every extreme that they name: `near_pairs`: each slot holds (receiving leaf, source leaf). The 32 slots of each device along leaf+rhs belong to receiving leaves among that device's 4 leaves; live pairs come first, the remaining slots are -1 in both columns. The source leaf lies within 4 leaves of the receiving one. In every draw some device has all its slots live. `local_lists`: each entry is -1 (unused) or the number, among the clusters of the same level counted from 0 in leaf order, of a cluster whose number differs from the listing cluster's by 2 or 3; entries of one list differ. `middle_lists`: as for the local lists, at the level of the subtree roots and the level below it. `upper_lists`: row h lists for heap cluster h (level t with 2^t <= h < 2^(t+1), number h - 2^t) as for the local lists; rows 0 to 3 are -1.
All inputs are finite; a program needn't handle non-finite values.
Results may differ from a plain program's by a relative error of at most 0.0003.
Values sent between devices are 32-bit elements; how exact they have to be, the bound alone decides.
A program may use at most 128 MiB of HBM per device.

v0:
```python
import jax
import jax.numpy as jnp
from jax import lax
from jax.sharding import PartitionSpec as P

NEAR_REACH = 4
highest = lax.Precision.HIGHEST


def with_halo(shard, sides, width):
    for axis, dim in sides:
        count, length = (lax.axis_size(axis), shard.shape[dim])
        up = [(i, (i + 1) % count) for i in range(count - 1)]
        down = [(j, i) for i, j in up]
        last = lax.slice_in_dim(shard, length - width, length, axis=dim)
        leading = lax.slice_in_dim(shard, 0, width, axis=dim)
        before = lax.ppermute(last, axis, up)
        after = lax.ppermute(leading, axis, down)
        shard = jnp.concatenate([before, shard, after], axis=dim)
    return shard


def lift_level(matrices, vectors):
    moved = jnp.einsum("nab,cna->cnb", matrices, vectors, precision=highest)
    return moved.reshape(moved.shape[0], moved.shape[1] // 2, 2, moved.shape[2]).sum(axis=2)


def couple_lists(blocks, positions, valid, table):
    clipped = jnp.clip(positions, 0, table.shape[1] - 1)
    picked = jnp.take(table, clipped, axis=1)
    picked = picked * valid.astype(table.dtype)[None, :, :, None]
    return jnp.einsum("nkab,cnkb->cna", blocks, picked, precision=highest)


def near_field(vectors_rows, near_blocks, near_pairs, first_leaf):
    extended = with_halo(vectors_rows, ((("leaf", "rhs"), 1),), NEAR_REACH)
    leaf_share = vectors_rows.shape[1]
    sources = jnp.clip(near_pairs[:, 1] - first_leaf + NEAR_REACH, 0, extended.shape[1] - 1)
    picked = jnp.take(extended, sources, axis=1)
    terms = jnp.einsum("pij,rpj->rpi", near_blocks, picked, precision=highest)
    targets = near_pairs[:, 0] - first_leaf
    owners = (targets[None, :] == jnp.arange(leaf_share, dtype=jnp.int32)[:, None]).astype(
        jnp.float32
    )
    return jnp.einsum("lp,rpi->rli", owners, terms, precision=highest)


def tree_pass(leaf_coeffs, group, groups, tree_data):
    (
        local_transfer,
        local_coupling,
        local_lists,
        middle_transfer,
        middle_coupling,
        middle_lists,
        upper_transfer,
        upper_coupling,
        upper_lists,
    ) = tree_data
    leaf_total = leaf_coeffs.shape[1]
    local_levels = leaf_total.bit_length() - 2
    top_depth = groups.bit_length() - 1
    amounts = [4 * 2**sublevel for sublevel in range(local_levels)]
    offsets = [4 * (2**sublevel - 1) for sublevel in range(local_levels)]
    upward = [leaf_coeffs] * local_levels
    for sublevel in range(local_levels - 1, 0, -1):
        start_row = offsets[sublevel]
        upward[sublevel - 1] = lift_level(
            local_transfer[start_row : start_row + amounts[sublevel]], upward[sublevel]
        )
    upper_pair = lift_level(local_transfer[0:4], upward[0])
    subtree_root = lift_level(middle_transfer, upper_pair)
    rims = jnp.stack(
        [
            jnp.concatenate([level_coeffs[:, :3], level_coeffs[:, -3:]], axis=1)
            for level_coeffs in upward
        ],
        axis=1,
    )
    bordered = with_halo(rims, (("leaf", 2),), 3)
    all_roots, all_pairs = (
        lax.all_gather(subtree_root, "leaf", axis=1, tiled=True),
        lax.all_gather(upper_pair, "leaf", axis=1, tiled=True),
    )
    climbing = {top_depth: all_roots}
    for tree_level in range(top_depth, 0, -1):
        lower_end = 2**tree_level
        climbing[tree_level - 1] = lift_level(
            upper_transfer[lower_end - 2 : 2 * lower_end - 2], climbing[tree_level]
        )
    numbered = jnp.concatenate(
        [jnp.zeros_like(climbing[0])] + [climbing[tree_level] for tree_level in range(top_depth)],
        axis=1,
    )
    level_start = jnp.int32(1)
    for exponent in range(1, top_depth):
        level_start = jnp.where(group >= 2**exponent, 2**exponent, level_start)
    owned_terms = couple_lists(
        upper_coupling, upper_lists + level_start, upper_lists >= 0, numbered
    )
    ancestor = lax.all_gather(owned_terms, "leaf", axis=1, tiled=True)
    descending = jnp.zeros_like(owned_terms[:, 0])
    for tree_level in range(1, top_depth):
        node_index = 2**tree_level + group // 2 ** (top_depth - tree_level)
        matrix = lax.dynamic_index_in_dim(upper_transfer, node_index - 2, 0, keepdims=False)
        descending = lax.dynamic_index_in_dim(ancestor, node_index, 1, keepdims=False) + jnp.einsum(
            "ab,cb->ca", matrix, descending, precision=highest
        )
    root_matrix = lax.dynamic_index_in_dim(upper_transfer, groups - 2 + group, 0, keepdims=False)
    root_lists = middle_lists[0:1]
    root_down = couple_lists(middle_coupling[0:1], root_lists, root_lists >= 0, all_roots)[
        :, 0
    ] + jnp.einsum("ab,cb->ca", root_matrix, descending, precision=highest)
    pair_lists = middle_lists[1:3]
    descending = couple_lists(
        middle_coupling[1:3], pair_lists, pair_lists >= 0, all_pairs
    ) + jnp.einsum("nab,cb->cna", middle_transfer, root_down, precision=highest)
    for sublevel in range(local_levels):
        amount = amounts[sublevel]
        offset = offsets[sublevel]
        extended = jnp.concatenate(
            [bordered[:, sublevel, :3], upward[sublevel], bordered[:, sublevel, 9:]], axis=1
        )
        entries = local_lists[offset : offset + amount]
        coupled = couple_lists(
            local_coupling[offset : offset + amount],
            entries - group * amount + 3,
            entries >= 0,
            extended,
        )
        descending = coupled + jnp.einsum(
            "nab,cnb->cna",
            local_transfer[offset : offset + amount],
            jnp.repeat(descending, 2, axis=1),
            precision=highest,
        )
    return descending


def apply_matrix(vectors_rows, near_blocks, near_pairs, leaf_basis, tree_data):
    group = lax.axis_index("leaf")
    groups = lax.axis_size("leaf")
    quarter = lax.axis_index("rhs")
    quarters = lax.axis_size("rhs")
    leaf_share = vectors_rows.shape[1]
    first_leaf = (group * quarters + quarter) * leaf_share
    near_part = near_field(vectors_rows, near_blocks, near_pairs, first_leaf)
    own_coeffs = jnp.einsum("lki,rli->rlk", leaf_basis, vectors_rows, precision=highest)
    leaf_coeffs = lax.all_gather(own_coeffs, "rhs", axis=1, tiled=True)
    descending = tree_pass(leaf_coeffs, group, groups, tree_data)
    own_rows = lax.dynamic_slice_in_dim(descending, quarter * leaf_share, leaf_share, 1)
    far_part = jnp.einsum("lki,rlk->rli", leaf_basis, own_rows, precision=highest)
    return near_part + far_part


def body(
    input_columns,
    near_blocks,
    near_pairs,
    leaf_basis,
    local_transfer,
    local_coupling,
    local_lists,
    middle_transfer,
    middle_coupling,
    middle_lists,
    upper_transfer,
    upper_coupling,
    upper_lists,
):
    tree_data = (
        local_transfer,
        local_coupling,
        local_lists,
        middle_transfer,
        middle_coupling,
        middle_lists,
        upper_transfer,
        upper_coupling,
        upper_lists,
    )
    vectors_rows = lax.all_to_all(input_columns, "rhs", split_axis=1, concat_axis=0, tiled=True)
    first_product = apply_matrix(vectors_rows, near_blocks, near_pairs, leaf_basis, tree_data)
    second_product = apply_matrix(first_product, near_blocks, near_pairs, leaf_basis, tree_data)
    return (first_product, second_product)


def solution(mesh):
    in_specs = (
        P("rhs", "leaf", None),
        P(("leaf", "rhs"), None, None),
        P(("leaf", "rhs"), None),
        P(("leaf", "rhs"), None, None),
        P("leaf", None, None),
        P("leaf", None, None, None),
        P("leaf", None),
        P("leaf", None, None),
        P("leaf", None, None, None),
        P("leaf", None),
        P(),
        P("leaf", None, None, None),
        P("leaf", None),
    )
    out_specs = (P(None, ("leaf", "rhs"), None), P(None, ("leaf", "rhs"), None))
    return jax.shard_map(body, mesh=mesh, in_specs=in_specs, out_specs=out_specs, check_vma=False)
```

profile of v0, /device:TPU:1, one launch (start us, length us, event | category | flops | bytes accessed | tf_op | source)
XLA Modules:
  0.0 549.1 jit_solution(10016394474385720229)
XLA Ops:
  2.1 5.0 all-to-all-start
  15.4 13.1 %constant_dynamic-slice_fusion.5 = (f32[1,64,64]{0,2,1:T(8,128)}, f32[1,64,64]{0,2,1:T(8,128)}, f32[1,64,64]{0,2,1:T(8,128)}, f32[1,64,64]{0,2,1:T(8,128)}, f32[1,64,64]{0,2,1:T(8,128)}, /*index=5*/f32[1,64,64]{0,2,1:T(8,128)}) fusion(f32[126,64,64]{0,2,1:T(8,128)} %param.35, s32[]{:T(128)S(6)} %select_n.163, s32[]{:T(128)S(6)} %select_n.162, ...), kind=kLoop, calls=%fused_computation.260 | loop fusion | bytes 196632 | tf_op jit(solution)/shard_map/jit(dynamic_index_in_dim)/dynamic_slice | solution.py:109
  46.1 4.3 copy.175
  50.4 3.4 copy.176
  53.7 3.0 copy.177
  63.2 3.0 copy.182
  67.5 3.0 copy.184
  70.6 2.9 copy.185
  82.6 9.6 %all_gather.24 = f32[8,16,64]{2,0,1:T(8,128)S(1)} all-gather(f32[8,4,64]{2,0,1:T(8,128)S(1)} %convolution_bitcast_fusion.7), channel_id=1, replica_groups=mesh['leaf'=64,'rhs'=4] {'rhs'}, dimensions={1}, use_global_device_ids=true | all-gather | bytes 40960 | tf_op jit(solution)/shard_map/all_gather | solution.py:149
  95.1 3.1 collective-permute-start
  98.2 7.9 %collective-permute-start.1 = (f32[8,4,256]{2,0,1:T(8,128)}, f32[8,4,256]{2,0,1:T(8,128)}, u32[]{:S(2)}, u32[]{:S(2)}) collective-permute-start(f32[8,4,256]{2,0,1:T(8,128)} %all_to_all.16), channel_id=1, source_target_pairs={{1,0},{2,1},{3,2},{4,3},{5,4},{6,5},{7,6},{8,7},{9,8},{10,9},{11,1... | collective-permute-start | bytes 98312 | tf_op jit(solution)/shard_map/ppermute | solution.py:18
  106.2 58.5 %all_gather.25 = f32[8,128,64]{2,0,1:T(8,128)} all-gather(f32[8,2,64]{2,0,1:T(8,128)S(1)} %bitcast_reduce_fusion.15), channel_id=1, replica_groups=mesh['leaf'=64,'rhs'=4] {'leaf'}, dimensions={1}, use_global_device_ids=true | all-gather | bytes 266240 | tf_op jit(solution)/shard_map/all_gather | solution.py:83
  165.8 43.2 %all-gather.4 = f32[64,64,8]{1,2,0:T(8,128)S(1)} all-gather(f32[1,64,8]{1,2,0:T(8,128)S(1)} %convolution_bitcast_fusion.19), channel_id=2, replica_groups=mesh['leaf'=64,'rhs'=4] {'leaf'}, dimensions={0}, use_global_device_ids=true | all-gather | bytes 133120 | tf_op jit(solution)/shard_map/all_gather | solution.py:82
  224.4 42.1 %all-gather.5 = f32[64,64,8]{1,2,0:T(8,128)S(1)} all-gather(f32[1,64,8]{1,2,0:T(8,128)S(1)} %convolution_bitcast_fusion.16), channel_id=3, replica_groups=mesh['leaf'=64,'rhs'=4] {'leaf'}, dimensions={0}, use_global_device_ids=true | all-gather | bytes 133120 | tf_op jit(solution)/shard_map/all_gather | solution.py:101
  312.6 3.6 fusion.4
  321.5 10.5 %convolution_bitcast_fusion.1 = f32[8,32,256]{2,0,1:T(8,128)S(1)} fusion(f32[32,256,256]{2,1,0:T(8,128)} %param.26, f32[32,8,256]{2,1,0:T(8,128)} %gather_fusion, pred[32]{0:T(512)(128)(4,1)S(1)} %copy-done.55), kind=kOutput, calls=%fused_computation.19 | convolution fusion | flops 201392128 | bytes 8912928 | tf_op jit(solution)/shard_map/pij,rpj->rpi/dot_general | solution.py:40
  333.9 9.6 %all_gather.28 = f32[8,16,64]{2,0,1:T(8,128)S(1)} all-gather(f32[8,4,64]{2,0,1:T(8,128)S(1)} %convolution_bitcast_fusion.6), channel_id=1, replica_groups=mesh['leaf'=64,'rhs'=4] {'rhs'}, dimensions={1}, use_global_device_ids=true | all-gather | bytes 40960 | tf_op jit(solution)/shard_map/all_gather | solution.py:149
  347.2 48.4 %all-gather.6 = f32[64,64,8]{1,2,0:T(8,128)S(1)} all-gather(f32[1,64,8]{1,2,0:T(8,128)S(1)} %convolution_bitcast_fusion.15), channel_id=4, replica_groups=mesh['leaf'=64,'rhs'=4] {'leaf'}, dimensions={0}, use_global_device_ids=true | all-gather | bytes 133120 | tf_op jit(solution)/shard_map/all_gather | solution.py:82
  403.0 47.4 %all_gather.29 = f32[8,128,64]{2,0,1:T(8,128)S(1)} all-gather(f32[8,2,64]{2,0,1:T(8,128)S(1)} %copy-done.37), channel_id=1, replica_groups=mesh['leaf'=64,'rhs'=4] {'leaf'}, dimensions={1}, use_global_device_ids=true | all-gather | bytes 266240 | tf_op jit(solution)/shard_map/all_gather | solution.py:83
  452.3 4.9 collective-permute-start.5
  457.3 4.3 collective-permute-start.6
  472.3 48.5 %all-gather.7 = f32[64,64,8]{1,2,0:T(8,128)S(1)} all-gather(f32[1,64,8]{1,2,0:T(8,128)S(1)} %convolution_bitcast_fusion.12), channel_id=5, replica_groups=mesh['leaf'=64,'rhs'=4] {'leaf'}, dimensions={0}, use_global_device_ids=true | all-gather | bytes 133120 | tf_op jit(solution)/shard_map/all_gather | solution.py:101
  526.4 3.5 fusion.7
  538.7 9.3 %convolution_bitcast_fusion = f32[8,32,256]{2,0,1:T(8,128)S(1)} fusion(f32[32,256,256]{2,1,0:T(8,128)} %param.26, f32[32,8,256]{2,1,0:T(8,128)S(1)} %gather_fusion.7, pred[32]{0:T(512)(128)(4,1)S(1)} %copy-done.56), kind=kOutput, calls=%fused_computation.18 | convolution fusion | flops 201392128 | bytes 8912928 | tf_op jit(solution)/shard_map/pij,rpj->rpi/dot_general | solution.py:40
  (313 shorter events, 155.4 us)
Async XLA Ops:
  0.6 80.8 %copy-start = (f32[4,64,256]{2,1,0:T(8,128)S(1)}, f32[4,64,256]{2,1,0:T(8,128)}, u32[]{:S(2)}) copy-start(f32[4,64,256]{2,1,0:T(8,128)} %param.28) | copy-start | bytes 786436
  2.1 77.9 %all-to-all-start = ((f32[2,16,256]{2,0,1:T(2,128)}), f32[2,16,256]{2,0,1:T(2,128)}, u32[]{:S(2)}, u32[]{:S(2)}) async-start(f32[2,16,256]{2,0,1:T(2,128)} %copy.124), calls=%async_computation | async-start | bytes 65536 | tf_op jit(solution)/shard_map/all_to_all | solution.py:182
  81.4 133.6 %copy-start.2 = (f32[64,64,64]{2,1,0:T(8,128)S(1)}, f32[64,64,64]{2,1,0:T(8,128)}, u32[]{:S(2)}) copy-start(f32[64,64,64]{2,1,0:T(8,128)} %copy.175) | copy-start | bytes 3145732
  92.2 72.5 %copy-start.16 = (f32[8,16,64]{2,0,1:T(8,128)}, f32[8,16,64]{2,0,1:T(8,128)S(1)}, u32[]{:S(2)}) copy-start(f32[8,16,64]{2,0,1:T(8,128)S(1)} %all_gather.24) | copy-start | bytes 98308
  92.7 72.0 %copy-start.25 = (f32[8,8,64]{2,0,1:T(8,128)}, f32[8,8,64]{2,0,1:T(8,128)S(1)}, u32[]{:S(2)}) copy-start(f32[8,8,64]{2,0,1:T(8,128)S(1)} %bitcast_reduce_fusion.7) | copy-start | bytes 49156
  95.1 222.6 %collective-permute-start = (f32[8,4,256]{2,0,1:T(8,128)}, f32[8,4,256]{2,0,1:T(8,128)}, u32[]{:S(2)}, u32[]{:S(2)}) collective-permute-start(f32[8,4,256]{2,0,1:T(8,128)} %all_to_all.16), channel_id=1, source_target_pairs={{0,1},{1,2},{2,3},{3,4},{4,5},{5,6},{6,7},{7,8},{8,9},{9,10},{10,1... | collective-permute-start | bytes 98312 | tf_op jit(solution)/shard_map/ppermute | solution.py:17
  98.2 219.5 %collective-permute-start.1 = (f32[8,4,256]{2,0,1:T(8,128)}, f32[8,4,256]{2,0,1:T(8,128)}, u32[]{:S(2)}, u32[]{:S(2)}) collective-permute-start(f32[8,4,256]{2,0,1:T(8,128)} %all_to_all.16), channel_id=1, source_target_pairs={{1,0},{2,1},{3,2},{4,3},{5,4},{6,5},{7,6},{8,7},{9,8},{10,9},{11,1... | collective-permute-start | bytes 98312 | tf_op jit(solution)/shard_map/ppermute | solution.py:18
  272.8 19.5 %collective-permute-start.2 = (f32[8,3,3,64]{3,0,2,1:T(8,128)}, f32[8,3,3,64]{3,0,2,1:T(8,128)}, u32[]{:S(2)}, u32[]{:S(2)}) collective-permute-start(f32[8,3,3,64]{3,0,2,1:T(8,128)} %get-tuple-element.38), channel_id=1, source_target_pairs={{0,4},{4,8},{8,12},{12,16},{16,20},{20,24},{24,28},{28,32},{32,36}... | collective-permute-start | bytes 55304 | tf_op jit(solution)/shard_map/ppermute | solution.py:17
  275.3 18.3 %collective-permute-start.3 = (f32[8,3,3,64]{3,0,2,1:T(8,128)}, f32[8,3,3,64]{3,0,2,1:T(8,128)}, u32[]{:S(2)}, u32[]{:S(2)}) collective-permute-start(f32[8,3,3,64]{3,0,2,1:T(8,128)} %get-tuple-element.39), channel_id=1, source_target_pairs={{4,0},{8,4},{12,8},{16,12},{20,16},{24,20},{28,24},{32,28},{36,32}... | collective-permute-start | bytes 55304 | tf_op jit(solution)/shard_map/ppermute | solution.py:18
  399.8 63.9 %copy-start.5 = (f32[32,64,64]{2,1,0:T(8,128)S(1)}, f32[32,64,64]{2,1,0:T(8,128)}, u32[]{:S(2)}) copy-start(f32[32,64,64]{2,1,0:T(8,128)} %copy.176) | copy-start | bytes 1572868
  399.8 64.8 %copy-start.9 = (f32[16,64,64]{2,1,0:T(8,128)S(1)}, f32[16,64,64]{2,1,0:T(8,128)}, u32[]{:S(2)}) copy-start(f32[16,64,64]{2,1,0:T(8,128)} %copy.177) | copy-start | bytes 786436
  402.8 62.8 %copy-start.13 = (f32[4,64,64]{2,1,0:T(8,128)S(1)}, f32[4,64,64]{2,1,0:T(8,128)}, u32[]{:S(2)}) copy-start(f32[4,64,64]{2,1,0:T(8,128)} %copy.179) | copy-start | bytes 196612
  402.8 63.0 %copy-start.21 = (f32[2,64,64]{2,1,0:T(8,128)S(1)}, f32[2,64,64]{2,1,0:T(8,128)}, u32[]{:S(2)}) copy-start(f32[2,64,64]{2,1,0:T(8,128)} %copy.180) | copy-start | bytes 98308
  403.0 68.4 %copy-start.22 = (f32[1,4,64,64]{3,2,1,0:T(8,128)S(1)}, f32[1,4,64,64]{3,2,1,0:T(8,128)}, u32[]{:S(2)}) copy-start(f32[1,4,64,64]{3,2,1,0:T(8,128)} %param.36) | copy-start | bytes 196612
  450.4 86.7 %collective-permute-start.4 = (f32[8,4,256]{2,1,0:T(4,128)}, f32[8,4,256]{2,1,0:T(4,128)}, u32[]{:S(2)}, u32[]{:S(2)}) collective-permute-start(f32[8,4,256]{2,1,0:T(4,128)} %fusion.13), channel_id=1, source_target_pairs={{0,1},{1,2},{2,3},{3,4},{4,5},{5,6},{6,7},{7,8},{8,9},{9,10},{10,1... | collective-permute-start | bytes 98312 | tf_op jit(solution)/shard_map/ppermute | solution.py:17
  452.3 84.8 %collective-permute-start.5 = (f32[8,4,256]{2,1,0:T(4,128)}, f32[8,4,256]{2,1,0:T(4,128)}, u32[]{:S(2)}, u32[]{:S(2)}) collective-permute-start(f32[8,4,256]{2,1,0:T(4,128)} %fusion.13), channel_id=1, source_target_pairs={{1,0},{2,1},{3,2},{4,3},{5,4},{6,5},{7,6},{8,7},{9,8},{10,9},{11,1... | collective-permute-start | bytes 98312 | tf_op jit(solution)/shard_map/ppermute | solution.py:18
  457.3 68.3 %collective-permute-start.6 = (f32[8,3,3,64]{3,0,2,1:T(8,128)S(1)}, f32[8,3,3,64]{3,0,2,1:T(8,128)S(1)}, u32[]{:S(2)}, u32[]{:S(2)}) collective-permute-start(f32[8,3,3,64]{3,0,2,1:T(8,128)S(1)} %get-tuple-element.36), channel_id=1, source_target_pairs={{0,4},{4,8},{8,12},{12,16},{16,20},{20,24},{24,28},{28,32},{32,36}... | collective-permute-start | bytes 55304 | tf_op jit(solution)/shard_map/ppermute | solution.py:17
  461.6 64.1 %collective-permute-start.7 = (f32[8,3,3,64]{3,0,2,1:T(8,128)S(1)}, f32[8,3,3,64]{3,0,2,1:T(8,128)S(1)}, u32[]{:S(2)}, u32[]{:S(2)}) collective-permute-start(f32[8,3,3,64]{3,0,2,1:T(8,128)S(1)} %get-tuple-element.37), channel_id=1, source_target_pairs={{4,0},{8,4},{12,8},{16,12},{20,16},{24,20},{28,24},{32,28},{36,32}... | collective-permute-start | bytes 55304 | tf_op jit(solution)/shard_map/ppermute | solution.py:18
  464.7 60.4 %copy-start.26 = (f32[1,64,64]{2,1,0:T(8,128)S(1)}, f32[1,64,64]{2,1,0:T(8,128)}, u32[]{:S(2)}) copy-start(f32[1,64,64]{2,1,0:T(8,128)} %copy.186) | copy-start | bytes 49156
  464.7 60.6 %copy-start.15 = (f32[2,64,64]{2,1,0:T(8,128)S(1)}, f32[2,64,64]{2,1,0:T(8,128)}, u32[]{:S(2)}) copy-start(f32[2,64,64]{2,1,0:T(8,128)} %param.32) | copy-start | bytes 98308
  465.3 60.4 %copy-start.19 = (f32[8,16,64]{2,0,1:T(8,128)S(1)}, f32[8,16,64]{2,0,1:T(8,128)}, u32[]{:S(2)}) copy-start(f32[8,16,64]{2,0,1:T(8,128)} %copy-done.18) | copy-start | bytes 98308
  465.3 60.5 %copy-start.33 = (s32[1024]{0:T(1024)S(1)}, s32[1024]{0:T(1024)}, u32[]{:S(2)}) copy-start(s32[1024]{0:T(1024)} %get-tuple-element.74) | copy-start | bytes 12292
  465.8 60.6 %copy-start.35 = (f32[16,4]{1,0:T(8,128)S(1)}, f32[16,4]{1,0:T(8,128)}, u32[]{:S(2)}) copy-start(f32[16,4]{1,0:T(8,128)} %copy.129) | copy-start | bytes 772
  465.8 60.6 %copy-start.52 = (pred[16,4]{1,0:T(8,128)(4,1)S(1)}, pred[16,4]{1,0:T(8,128)(4,1)}, u32[]{:S(2)}) copy-start(pred[16,4]{1,0:T(8,128)(4,1)} %copy.127) | copy-start | bytes 196
  (49 other events, 1024.3 us)
where the time goes:
time: 558 us; the launch traced here: 549 us
  blocking collectives  307 us (55%)
  local copies, waits for them, and re-layouts  114 us (20%)
  matrix products  74.3 us (13%)
  starting transfers between devices  34.3 us (6%)
  other arithmetic  17.7 us (3%)
    all_gather x2, blocking collectives, tree_pass(): lax.all_gather(upper_pair, 'leaf', axis=1, tiled=True)  106 us
    all_gather x2, blocking collectives, tree_pass(): lax.all_gather(subtree_root, 'leaf', axis=1, tiled=True)  91.6 us
    all_gather x2, blocking collectives, tree_pass(): ancestor = lax.all_gather(owned_terms, 'leaf', axis=1, tiled=True)  90.5 us
    unnamed x155, local copies, waits for them, and re-layouts  43 us
    dot_general x12, matrix products, couple_lists(): return jnp.einsum('nkab,cnkb->cna', blocks, picked, precision=highest)  21.4 us
    dot_general x2, matrix products, near_field(): terms = jnp.einsum('pij,rpj->rpi', near_blocks, picked, precision=highest)  19.8 us
    all_gather x2, blocking collectives, apply_matrix(): leaf_coeffs = lax.all_gather(own_coeffs, 'rhs', axis=1, tiled=True)  19.1 us
    gather x12, local copies, waits for them, and re-layouts, couple_lists(): picked = jnp.take(table, clipped, axis=1)  18.1 us
  transfers between devices with their start and end apart: 9, of which 1 were waited for; matrix products, arithmetic and copies ran while one was open for 29% of the time, Pallas kernels for 0%

commit v1 on v0

--- a/solution.py
+++ b/solution.py
@@ -78,9 +78,18 @@
         axis=1,
     )
     bordered = with_halo(rims, (("leaf", 2),), 3)
+    _make_counts = lambda t0: jnp.concatenate(
+        jax.lax.all_to_all(
+            jnp.stack([t0 for _ in range(jax.lax.axis_size("leaf"))]),
+            axis_name="leaf",
+            split_axis=0,
+            concat_axis=0,
+        ),
+        axis=1,
+    )
     all_roots, all_pairs = (
         lax.all_gather(subtree_root, "leaf", axis=1, tiled=True),
-        lax.all_gather(upper_pair, "leaf", axis=1, tiled=True),
+        _make_counts(upper_pair),
     )
     climbing = {top_depth: all_roots}
     for tree_level in range(top_depth, 0, -1):

time: 558 us -> 480 us (0.86)
  blocking collectives: 307 us -> 206 us
  starting transfers between devices: 34.3 us -> 48.3 us
    all_gather x2 -> x0, blocking collectives: 106 us -> none  [tree_pass(): lax.all_gather(upper_pair, 'leaf', axis=1, tiled=True)]
    all_to_all x0 -> x2, starting transfers between devices: none -> 14.5 us  [tree_pass(): jax.lax.all_to_all(jnp.stack([t0 for _ in range(jax.lax.axis_size('leaf')...]
    unnamed x155 -> x165, local copies, waits for them, and re-layouts: 43 us -> 48.7 us
  transfers between devices with their start and end apart: 9 -> 11, of which waited for: 1 -> 0; matrix products, arithmetic and copies ran while one was open for 29% -> 37% of each run, Pallas kernels for 0% -> 0%
where the time goes in v1:
time: 480 us; the launch traced here: 470 us
  blocking collectives  206 us (43%)
  local copies, waits for them, and re-layouts  119 us (25%)
  matrix products  73.3 us (15%)
  starting transfers between devices  48.3 us (10%)
  other arithmetic  21.9 us (5%)
    all_gather x2, blocking collectives, tree_pass(): lax.all_gather(subtree_root, 'leaf', axis=1, tiled=True)  97.1 us
    all_gather x2, blocking collectives, tree_pass(): ancestor = lax.all_gather(owned_terms, 'leaf', axis=1, tiled=True)  90.6 us
    unnamed x165, local copies, waits for them, and re-layouts  48.7 us
    dot_general x12, matrix products, couple_lists(): return jnp.einsum('nkab,cnkb->cna', blocks, picked, precision=highest)  20.6 us
    dot_general x2, matrix products, near_field(): terms = jnp.einsum('pij,rpj->rpi', near_blocks, picked, precision=highest)  20.5 us
    all_gather x2, blocking collectives, apply_matrix(): leaf_coeffs = lax.all_gather(own_coeffs, 'rhs', axis=1, tiled=True)  18.5 us
    gather x12, local copies, waits for them, and re-layouts, couple_lists(): picked = jnp.take(table, clipped, axis=1)  18.1 us
    ppermute x4, starting transfers between devices, with_halo(): after = lax.ppermute(leading, axis, down)  17.2 us
  transfers between devices with their start and end apart: 11, of which 0 were waited for; matrix products, arithmetic and copies ran while one was open for 37% of the time, Pallas kernels for 0%

profile of v1, /device:TPU:1, one launch (start us, length us, event | category | flops | bytes accessed | tf_op | source)
XLA Modules:
  0.0 470.5 jit_solution(8486787094770459709)
XLA Ops:
  2.1 5.0 %all-to-all-start = ((f32[2,16,256]{2,0,1:T(2,128)}), f32[2,16,256]{2,0,1:T(2,128)}, u32[]{:S(2)}, u32[]{:S(2)}) async-start(f32[2,16,256]{2,0,1:T(2,128)} %copy.126), calls=%async_computation | async-start | bytes 65536 | tf_op jit(solution)/shard_map/all_to_all | solution.py:191
  14.0 13.1 %constant_dynamic-slice_fusion.5 = (f32[1,64,64]{0,2,1:T(8,128)}, f32[1,64,64]{0,2,1:T(8,128)}, f32[1,64,64]{0,2,1:T(8,128)}, f32[1,64,64]{0,2,1:T(8,128)}, f32[1,64,64]{0,2,1:T(8,128)}, /*index=5*/f32[1,64,64]{0,2,1:T(8,128)}) fusion(f32[126,64,64]{0,2,1:T(8,128)} %param.35, s32[]{:T(128)S(6)} %select_n.163, s32[]{:T(128)S(6)} %select_n.162, ...), kind=kLoop, calls=%fused_computation.260 | loop fusion | bytes 196632 | tf_op jit(solution)/shard_map/jit(dynamic_index_in_dim)/dynamic_slice | solution.py:118
  45.4 3.9 copy.177
  49.3 3.4 copy.178
  52.7 3.0 copy.179
  62.2 3.0 copy.184
  66.5 3.0 copy.186
  81.7 9.6 %all_gather.18 = f32[8,16,64]{2,0,1:T(8,128)S(1)} all-gather(f32[8,4,64]{2,0,1:T(8,128)S(1)} %convolution_bitcast_fusion.7), channel_id=1, replica_groups=mesh['leaf'=64,'rhs'=4] {'rhs'}, dimensions={1}, use_global_device_ids=true | all-gather | bytes 40960 | tf_op jit(solution)/shard_map/all_gather | solution.py:158
  94.1 3.1 collective-permute-start
  97.2 7.9 %collective-permute-start.1 = (f32[8,4,256]{2,0,1:T(8,128)}, f32[8,4,256]{2,0,1:T(8,128)}, u32[]{:S(2)}, u32[]{:S(2)}) collective-permute-start(f32[8,4,256]{2,0,1:T(8,128)} %all_to_all.22), channel_id=1, source_target_pairs={{1,0},{2,1},{3,2},{4,3},{5,4},{6,5},{7,6},{8,7},{9,8},{10,9},{11,1... | collective-permute-start | bytes 98312 | tf_op jit(solution)/shard_map/ppermute | solution.py:18
  107.1 47.9 %all-gather.4 = f32[64,64,8]{1,2,0:T(8,128)S(1)} all-gather(f32[1,64,8]{1,2,0:T(8,128)S(1)} %convolution_bitcast_fusion.19), channel_id=2, replica_groups=mesh['leaf'=64,'rhs'=4] {'leaf'}, dimensions={0}, use_global_device_ids=true | all-gather | bytes 133120 | tf_op jit(solution)/shard_map/all_gather | solution.py:91
  170.4 43.1 %all-gather.5 = f32[64,64,8]{1,2,0:T(8,128)S(1)} all-gather(f32[1,64,8]{1,2,0:T(8,128)S(1)} %convolution_bitcast_fusion.16), channel_id=3, replica_groups=mesh['leaf'=64,'rhs'=4] {'leaf'}, dimensions={0}, use_global_device_ids=true | all-gather | bytes 133120 | tf_op jit(solution)/shard_map/all_gather | solution.py:110
  219.8 7.4 %all-to-all-start.1 = ((f32[64,1,1024]{2,1,0:T(1,128)}), f32[64,1,1024]{2,1,0:T(1,128)}, u32[]{:S(2)}, u32[]{:S(2)}) async-start(f32[64,1,1024]{2,1,0:T(1,128)} %reshape.441), calls=%async_computation.1 | async-start | bytes 524288 | tf_op jit(solution)/shard_map/all_to_all | solution.py:82
  229.3 3.5 collective-permute-start.2
  260.5 4.2 fusion.4
  270.1 11.1 %convolution_bitcast_fusion.1 = f32[8,32,256]{2,0,1:T(8,128)} fusion(f32[32,256,256]{2,1,0:T(8,128)} %param.26, f32[32,8,256]{2,1,0:T(8,128)} %gather_fusion, pred[32]{0:T(512)(128)(4,1)} %get-tuple-element.18), kind=kOutput, calls=%fused_computation.19 | convolution fusion | flops 201392128 | bytes 8912928 | tf_op jit(solution)/shard_map/pij,rpj->rpi/dot_general | solution.py:40
  297.0 9.0 %all_gather.21 = f32[8,16,64]{2,0,1:T(8,128)S(1)} all-gather(f32[8,4,64]{2,0,1:T(8,128)S(1)} %convolution_bitcast_fusion.6), channel_id=1, replica_groups=mesh['leaf'=64,'rhs'=4] {'rhs'}, dimensions={1}, use_global_device_ids=true | all-gather | bytes 40960 | tf_op jit(solution)/shard_map/all_gather | solution.py:158
  309.7 49.3 %all-gather.6 = f32[64,64,8]{1,2,0:T(8,128)S(1)} all-gather(f32[1,64,8]{1,2,0:T(8,128)S(1)} %convolution_bitcast_fusion.15), channel_id=4, replica_groups=mesh['leaf'=64,'rhs'=4] {'leaf'}, dimensions={0}, use_global_device_ids=true | all-gather | bytes 133120 | tf_op jit(solution)/shard_map/all_gather | solution.py:91
  368.3 4.9 %collective-permute-start.5 = (f32[8,4,256]{2,1,0:T(4,128)}, f32[8,4,256]{2,1,0:T(4,128)S(1)}, u32[]{:S(2)}, u32[]{:S(2)}) collective-permute-start(f32[8,4,256]{2,1,0:T(4,128)} %fusion.13), channel_id=1, source_target_pairs={{1,0},{2,1},{3,2},{4,3},{5,4},{6,5},{7,6},{8,7},{9,8},{10,9},{11,1... | collective-permute-start | bytes 98312 | tf_op jit(solution)/shard_map/ppermute | solution.py:18
  373.3 3.1 collective-permute-start.6
  386.4 47.5 %all-gather.7 = f32[64,64,8]{1,2,0:T(8,128)S(1)} all-gather(f32[1,64,8]{1,2,0:T(8,128)S(1)} %convolution_bitcast_fusion.12), channel_id=5, replica_groups=mesh['leaf'=64,'rhs'=4] {'leaf'}, dimensions={0}, use_global_device_ids=true | all-gather | bytes 133120 | tf_op jit(solution)/shard_map/all_gather | solution.py:110
  436.2 7.1 %all-to-all-start.2 = ((f32[64,1,1024]{2,1,0:T(1,128)}), f32[64,1,1024]{2,1,0:T(1,128)S(1)}, u32[]{:S(2)}, u32[]{:S(2)}) async-start(f32[64,1,1024]{2,1,0:T(1,128)} %reshape.443), calls=%async_computation.2 | async-start | bytes 524288 | tf_op jit(solution)/shard_map/all_to_all | solution.py:82
  445.0 3.5 fusion.7
  455.2 9.3 %convolution_bitcast_fusion = f32[8,32,256]{2,0,1:T(8,128)S(1)} fusion(f32[32,256,256]{2,1,0:T(8,128)} %param.26, f32[32,8,256]{2,1,0:T(8,128)S(1)} %gather_fusion.7, pred[32]{0:T(512)(128)(4,1)S(1)} %copy-done.56), kind=kOutput, calls=%fused_computation.18 | convolution fusion | flops 201392128 | bytes 8912928 | tf_op jit(solution)/shard_map/pij,rpj->rpi/dot_general | solution.py:40
  (328 shorter events, 162.7 us)
Async XLA Ops:
  0.6 79.8 %copy-start = (f32[4,64,256]{2,1,0:T(8,128)S(1)}, f32[4,64,256]{2,1,0:T(8,128)}, u32[]{:S(2)}) copy-start(f32[4,64,256]{2,1,0:T(8,128)} %param.28) | copy-start | bytes 786436
  2.1 76.9 %all-to-all-start = ((f32[2,16,256]{2,0,1:T(2,128)}), f32[2,16,256]{2,0,1:T(2,128)}, u32[]{:S(2)}, u32[]{:S(2)}) async-start(f32[2,16,256]{2,0,1:T(2,128)} %copy.126), calls=%async_computation | async-start | bytes 65536 | tf_op jit(solution)/shard_map/all_to_all | solution.py:191
  80.4 80.6 %copy-start.2 = (f32[64,64,64]{2,1,0:T(8,128)S(1)}, f32[64,64,64]{2,1,0:T(8,128)}, u32[]{:S(2)}) copy-start(f32[64,64,64]{2,1,0:T(8,128)} %copy.177) | copy-start | bytes 3145732
  94.1 172.2 %collective-permute-start = (f32[8,4,256]{2,0,1:T(8,128)}, f32[8,4,256]{2,0,1:T(8,128)}, u32[]{:S(2)}, u32[]{:S(2)}) collective-permute-start(f32[8,4,256]{2,0,1:T(8,128)} %all_to_all.22), channel_id=1, source_target_pairs={{0,1},{1,2},{2,3},{3,4},{4,5},{5,6},{6,7},{7,8},{8,9},{9,10},{10,1... | collective-permute-start | bytes 98312 | tf_op jit(solution)/shard_map/ppermute | solution.py:17
  97.2 169.1 %collective-permute-start.1 = (f32[8,4,256]{2,0,1:T(8,128)}, f32[8,4,256]{2,0,1:T(8,128)}, u32[]{:S(2)}, u32[]{:S(2)}) collective-permute-start(f32[8,4,256]{2,0,1:T(8,128)} %all_to_all.22), channel_id=1, source_target_pairs={{1,0},{2,1},{3,2},{4,3},{5,4},{6,5},{7,6},{8,7},{9,8},{10,9},{11,1... | collective-permute-start | bytes 98312 | tf_op jit(solution)/shard_map/ppermute | solution.py:18
  219.8 61.5 %all-to-all-start.1 = ((f32[64,1,1024]{2,1,0:T(1,128)}), f32[64,1,1024]{2,1,0:T(1,128)}, u32[]{:S(2)}, u32[]{:S(2)}) async-start(f32[64,1,1024]{2,1,0:T(1,128)} %reshape.441), calls=%async_computation.1 | async-start | bytes 524288 | tf_op jit(solution)/shard_map/all_to_all | solution.py:82
  229.3 15.4 %collective-permute-start.2 = (f32[8,3,3,64]{3,0,2,1:T(8,128)}, f32[8,3,3,64]{3,0,2,1:T(8,128)}, u32[]{:S(2)}, u32[]{:S(2)}) collective-permute-start(f32[8,3,3,64]{3,0,2,1:T(8,128)} %get-tuple-element.38), channel_id=1, source_target_pairs={{0,4},{4,8},{8,12},{12,16},{16,20},{20,24},{24,28},{28,32},{32,36}... | collective-permute-start | bytes 55304 | tf_op jit(solution)/shard_map/ppermute | solution.py:17
  232.9 13.3 %collective-permute-start.3 = (f32[8,3,3,64]{3,0,2,1:T(8,128)}, f32[8,3,3,64]{3,0,2,1:T(8,128)}, u32[]{:S(2)}, u32[]{:S(2)}) collective-permute-start(f32[8,3,3,64]{3,0,2,1:T(8,128)} %get-tuple-element.39), channel_id=1, source_target_pairs={{4,0},{8,4},{12,8},{16,12},{20,16},{24,20},{28,24},{32,28},{36,32}... | collective-permute-start | bytes 55304 | tf_op jit(solution)/shard_map/ppermute | solution.py:18
  366.4 87.2 %collective-permute-start.4 = (f32[8,4,256]{2,1,0:T(4,128)}, f32[8,4,256]{2,1,0:T(4,128)S(1)}, u32[]{:S(2)}, u32[]{:S(2)}) collective-permute-start(f32[8,4,256]{2,1,0:T(4,128)} %fusion.13), channel_id=1, source_target_pairs={{0,1},{1,2},{2,3},{3,4},{4,5},{5,6},{6,7},{7,8},{8,9},{9,10},{10,1... | collective-permute-start | bytes 98312 | tf_op jit(solution)/shard_map/ppermute | solution.py:17
  368.3 85.3 %collective-permute-start.5 = (f32[8,4,256]{2,1,0:T(4,128)}, f32[8,4,256]{2,1,0:T(4,128)S(1)}, u32[]{:S(2)}, u32[]{:S(2)}) collective-permute-start(f32[8,4,256]{2,1,0:T(4,128)} %fusion.13), channel_id=1, source_target_pairs={{1,0},{2,1},{3,2},{4,3},{5,4},{6,5},{7,6},{8,7},{9,8},{10,9},{11,1... | collective-permute-start | bytes 98312 | tf_op jit(solution)/shard_map/ppermute | solution.py:18
  373.3 70.9 %collective-permute-start.6 = (f32[8,3,3,64]{3,0,2,1:T(8,128)S(1)}, f32[8,3,3,64]{3,0,2,1:T(8,128)S(1)}, u32[]{:S(2)}, u32[]{:S(2)}) collective-permute-start(f32[8,3,3,64]{3,0,2,1:T(8,128)S(1)} %get-tuple-element.36), channel_id=1, source_target_pairs={{0,4},{4,8},{8,12},{12,16},{16,20},{20,24},{24,28},{28,32},{32,36}... | collective-permute-start | bytes 55304 | tf_op jit(solution)/shard_map/ppermute | solution.py:17
  376.4 58.5 %copy-start.11 = (f32[3,4,64,64]{3,2,1,0:T(8,128)S(1)}, f32[3,4,64,64]{3,2,1,0:T(8,128)}, u32[]{:S(2)}) copy-start(f32[3,4,64,64]{3,2,1,0:T(8,128)} %param.33) | copy-start | bytes 589828
  376.5 67.8 %collective-permute-start.7 = (f32[8,3,3,64]{3,0,2,1:T(8,128)S(1)}, f32[8,3,3,64]{3,0,2,1:T(8,128)S(1)}, u32[]{:S(2)}, u32[]{:S(2)}) collective-permute-start(f32[8,3,3,64]{3,0,2,1:T(8,128)S(1)} %get-tuple-element.37), channel_id=1, source_target_pairs={{4,0},{8,4},{12,8},{16,12},{20,16},{24,20},{28,24},{32,28},{36,32}... | collective-permute-start | bytes 55304 | tf_op jit(solution)/shard_map/ppermute | solution.py:18
  380.4 63.0 %copy-start.30 = (f32[1,64,64]{2,1,0:T(8,128)S(1)}, f32[1,64,64]{2,1,0:T(8,128)}, u32[]{:S(2)}) copy-start(f32[1,64,64]{2,1,0:T(8,128)} %copy.184) | copy-start | bytes 49156
  380.4 63.0 %copy-start.46 = (f32[8,64]{1,0:T(8,128)S(1)}, f32[8,64]{1,0:T(8,128)}, u32[]{:S(2)}) copy-start(f32[8,64]{1,0:T(8,128)} %fusion.90) | copy-start | bytes 6148
  380.4 63.2 %copy-start.29 = (f32[1,64,64]{2,1,0:T(8,128)S(1)}, f32[1,64,64]{2,1,0:T(8,128)}, u32[]{:S(2)}) copy-start(f32[1,64,64]{2,1,0:T(8,128)} %copy.185) | copy-start | bytes 49156
  380.4 63.3 %copy-start.28 = (f32[1,64,64]{2,1,0:T(8,128)S(1)}, f32[1,64,64]{2,1,0:T(8,128)}, u32[]{:S(2)}) copy-start(f32[1,64,64]{2,1,0:T(8,128)} %copy.186) | copy-start | bytes 49156
  380.4 63.5 %copy-start.27 = (f32[1,64,64]{2,1,0:T(8,128)S(1)}, f32[1,64,64]{2,1,0:T(8,128)}, u32[]{:S(2)}) copy-start(f32[1,64,64]{2,1,0:T(8,128)} %copy.187) | copy-start | bytes 49156
  380.4 63.7 %copy-start.26 = (f32[1,64,64]{2,1,0:T(8,128)S(1)}, f32[1,64,64]{2,1,0:T(8,128)}, u32[]{:S(2)}) copy-start(f32[1,64,64]{2,1,0:T(8,128)} %copy.188) | copy-start | bytes 49156
  382.0 62.3 %copy-start.18 = (f32[8,16,64]{2,0,1:T(8,128)S(1)}, f32[8,16,64]{2,0,1:T(8,128)}, u32[]{:S(2)}) copy-start(f32[8,16,64]{2,0,1:T(8,128)} %copy-done.17) | copy-start | bytes 98308
  383.9 60.5 %copy-start.33 = (s32[1024]{0:T(1024)S(1)}, s32[1024]{0:T(1024)}, u32[]{:S(2)}) copy-start(s32[1024]{0:T(1024)} %get-tuple-element.74) | copy-start | bytes 12292
  386.4 58.6 %copy-start.35 = (f32[16,4]{1,0:T(8,128)S(1)}, f32[16,4]{1,0:T(8,128)}, u32[]{:S(2)}) copy-start(f32[16,4]{1,0:T(8,128)} %copy.131) | copy-start | bytes 772
  386.4 58.6 %copy-start.50 = (pred[16,4]{1,0:T(8,128)(4,1)S(1)}, pred[16,4]{1,0:T(8,128)(4,1)}, u32[]{:S(2)}) copy-start(pred[16,4]{1,0:T(8,128)(4,1)} %copy.129) | copy-start | bytes 196
  436.2 28.4 %all-to-all-start.2 = ((f32[64,1,1024]{2,1,0:T(1,128)}), f32[64,1,1024]{2,1,0:T(1,128)S(1)}, u32[]{:S(2)}, u32[]{:S(2)}) async-start(f32[64,1,1024]{2,1,0:T(1,128)} %reshape.443), calls=%async_computation.2 | async-start | bytes 524288 | tf_op jit(solution)/shard_map/all_to_all | solution.py:82
  (53 other events, 598.1 us)
